TPU v7x, 32 devices: a whole 2x2x4 slice. The times are simulated.
32 devices in a mesh: rows: 8 (over z, y), cols: 4 (over x, core).
Axes of the slice: x: 2, y: 2, z: 4, core: 2. Of those that a mesh axis runs over, the one named last changes fastest.
Arguments:
- feats_t: bfloat16 [128, 16384], P('cols', 'rows'), may hold values from -6 to 6
- adj_index: int32 [128, 16], replicated, may hold values from 0 to 127, as said below
- adj_weight: bfloat16 [128, 16, 128, 128], P('rows'), as said below
- weight: bfloat16 [128, 256], replicated, may hold values from -0.5 to 0.5
- cotangent_t: bfloat16 [256, 16384], P('cols', 'rows'), may hold values from -6 to 6
Outputs:
- output_t: bfloat16 [256, 16384], P('cols', 'rows')
- weight_grad: float32 [128, 256], P('cols')
- feat_grad: float32 [128, 16384], P('cols', 'rows')
Inputs may be any that keep to these rules, and one draw needn't show every extreme that they name: `adj_index`: slot 0 of row block i names block i itself. Blocks are grouped 16 to a device in order. Slot 1 names a block of the next device (device index plus one, cyclically). The row blocks of one device name at most 4 distinct blocks of any other device, and exactly 4 of the next one. A block may stand in several slots of one row block. `adj_weight`: Nonnegative; about one entry in eight is nonzero.
All inputs are finite; a program needn't handle non-finite values.
Results may differ from a plain program's by a relative error of at most 0.0054.
Values may be sent and summed in bfloat16 or wider, within the bound.
No kernel may reach another device: no remote copies, remote signals or barrier semaphores. Data moves between devices by JAX's collectives and lax.ppermute only.
A program may use at most 128 MiB of HBM per device.

v0:
```python
import math
import jax
import jax.numpy as jnp
from jax import lax
from jax.sharding import PartitionSpec as P

CAP = 4


def body(feats_t, adj_index, adj_weight, weight, cotangent_t):
    feat_rows, node_cols = feats_t.shape
    blocks_n = adj_weight.shape[0]
    slots_n = adj_weight.shape[1]
    tile_n = adj_weight.shape[2]
    row_devs = lax.axis_size("rows")
    row_pos = lax.axis_index("rows")
    col_pos = lax.axis_index("cols")
    unit_rows = cotangent_t.shape[0]
    own_index = lax.dynamic_slice_in_dim(adj_index, row_pos * blocks_n, blocks_n, 0)
    own_flat = own_index.reshape(-1)
    local_tiles = feats_t.reshape(feat_rows, blocks_n, tile_n).transpose(1, 0, 2)
    device_ids = jnp.arange(row_devs, dtype=jnp.int32)
    slot_ids = jnp.arange(CAP, dtype=jnp.int32)
    mine = row_pos * blocks_n + jnp.arange(blocks_n, dtype=jnp.int32)
    peers_index = adj_index.reshape(row_devs, blocks_n * slots_n)
    wanted = (
        jnp.any(peers_index[:, :, None] == mine[None, None, :], axis=1)
        & (device_ids != row_pos)[:, None]
    )
    ordinal = jnp.cumsum(wanted.astype(jnp.int32), axis=1) - 1
    selector = wanted[:, None, :] & (ordinal[:, None, :] == slot_ids[None, :, None])
    source = own_flat // blocks_n
    block_pos = own_flat % blocks_n
    needed = jnp.any(
        own_flat[:, None] == jnp.arange(row_devs * blocks_n, dtype=jnp.int32)[None, :], axis=0
    )
    needed = needed.reshape(row_devs, blocks_n) & (device_ids != row_pos)[:, None]
    need_order = jnp.cumsum(needed.astype(jnp.int32), axis=1) - 1
    slot_of = source * CAP + need_order.reshape(-1)[own_flat]
    remote = source != row_pos
    outgoing = jnp.einsum(
        "pcb,bfj->pcfj",
        selector.astype(jnp.bfloat16),
        local_tiles,
        preferred_element_type=jnp.float32,
    ).astype(jnp.bfloat16)
    incoming = lax.all_to_all(outgoing, "rows", split_axis=0, concat_axis=0, tiled=True)
    received = incoming.reshape(row_devs * CAP, feat_rows, tile_n)[slot_of]
    own_part = local_tiles[block_pos]
    picked = jnp.where(remote[:, None, None], received, own_part).reshape(
        blocks_n, slots_n, feat_rows, tile_n
    )
    aggregate = jnp.einsum("bkfj,bkij->fbi", picked, adj_weight, preferred_element_type=jnp.float32)
    aggregated = aggregate.reshape(feat_rows, node_cols).astype(jnp.bfloat16)
    w_slab = lax.dynamic_slice_in_dim(weight, col_pos * unit_rows, unit_rows, 1)
    pre_act = lax.dot_general(
        w_slab,
        lax.all_gather(aggregated, "cols", axis=0, tiled=True),
        (((0,), (0,)), ((), ())),
        preferred_element_type=jnp.float32,
    )
    output_t = jax.nn.silu(pre_act).astype(jnp.bfloat16)
    sigm = jax.nn.sigmoid(pre_act)
    pre_grad = (cotangent_t.astype(jnp.float32) * sigm * (1.0 + pre_act * (1.0 - sigm))).astype(
        jnp.bfloat16
    )
    w_mine = lax.dynamic_slice_in_dim(weight, col_pos * feat_rows, feat_rows, 0)
    portion = lax.all_gather(pre_grad, "cols", axis=0, tiled=True)
    grad_acc = jnp.dot(w_mine, portion, preferred_element_type=jnp.float32)
    block_grad = lax.dot_general(
        aggregated, portion, (((1,), (1,)), ((), ())), preferred_element_type=jnp.float32
    )
    grad_scale = 1.0 / math.sqrt(node_cols * row_devs)
    weight_grad = lax.psum(block_grad, "rows") * grad_scale
    agg_grad = grad_acc.astype(jnp.bfloat16)
    contrib = jnp.einsum(
        "fbi,bkij->bkfj",
        agg_grad.reshape(feat_rows, blocks_n, tile_n),
        adj_weight,
        preferred_element_type=jnp.float32,
    )
    contrib_flat = contrib.reshape(blocks_n * slots_n, feat_rows * tile_n)
    slot_total = row_devs * CAP
    send_target = jnp.where(remote, slot_of, slot_total)
    sending = jax.ops.segment_sum(contrib_flat, send_target, num_segments=slot_total + 1)[
        :slot_total
    ]
    sending = sending.reshape(row_devs, CAP, feat_rows, tile_n)
    arrived = lax.all_to_all(
        sending.astype(jnp.bfloat16), "rows", split_axis=0, concat_axis=0, tiled=True
    ).astype(sending.dtype)
    arrived_flat = arrived.reshape(slot_total, feat_rows * tile_n)
    block_ids = jnp.arange(blocks_n, dtype=jnp.int32)
    slot_block = jnp.sum(selector.astype(jnp.int32) * block_ids[None, None, :], axis=2)
    slot_used = jnp.any(selector, axis=2)
    peer_target = jnp.where(slot_used, slot_block, blocks_n).reshape(-1)
    from_peers = jax.ops.segment_sum(arrived_flat, peer_target, num_segments=blocks_n + 1)[
        :blocks_n
    ]
    self_target = jnp.where(remote, blocks_n, block_pos)
    from_self = jax.ops.segment_sum(contrib_flat, self_target, num_segments=blocks_n + 1)[:blocks_n]
    summed = (from_peers + from_self).reshape(blocks_n, feat_rows, tile_n)
    feat_grad = summed.transpose(1, 0, 2).reshape(feat_rows, node_cols)
    return (output_t, weight_grad, feat_grad)


def solution(mesh):
    return jax.shard_map(
        body,
        mesh=mesh,
        in_specs=(P("cols", "rows"), P(), P("rows", None, None, None), P(), P("cols", "rows")),
        out_specs=(P("cols", "rows"), P("cols", None), P("cols", "rows")),
        check_vma=False,
    )
```

profile of v0, /device:TPU:0, one launch (start us, length us, event | category | flops | bytes accessed | tf_op | source)
XLA Modules:
  0.0 143.8 jit_solution(9876244328487271256)
XLA Ops:
  7.2 0.8 copy.41
  8.0 0.8 fusion.39
  8.9 0.1 fusion.30
  9.3 0.3 compare_reduce_fusion
  9.6 0.2 reduce_window_sum.17
  9.8 0.9 copy.60
  10.7 0.2 convolution_convert_fusion.1
  10.9 0.7 copy.44
  11.7 7.3 %all-to-all-start = ((bf16[8,4,32,128]{3,2,1,0:T(8,128)(2,1)}), bf16[8,4,32,128]{3,2,1,0:T(8,128)(2,1)S(1)}, u32[]{:S(2)}, u32[]{:S(2)}) async-start(bf16[8,4,32,128]{3,2,1,0:T(8,128)(2,1)} %copy.44), calls=%async_computation | async-start | bytes 524288 | tf_op jit(solution)/shard_map/all_to_all | solution.py:47
  19.1 0.2 reduce_window_sum.18
  19.4 1.9 %gather_fusion = s32[256]{0:T(256)S(1)} fusion(s32[128]{0:T(128)S(1)} %sub.23, s32[1024]{0:T(1024)S(1)} %pad_clamp_fusion.2), kind=kCustom, calls=%fused_computation | custom fusion | bytes 3072 | tf_op jit(solution)/shard_map/gather | solution.py:39
  21.4 0.9 bitcast_bitcast_fusion
  22.3 1.0 gather_fusion.2
  23.4 4.6 %all-to-all-done = bf16[8,4,32,128]{3,2,1,0:T(8,128)(2,1)S(1)} async-done(((bf16[8,4,32,128]{3,2,1,0:T(8,128)(2,1)}), bf16[8,4,32,128]{3,2,1,0:T(8,128)(2,1)S(1)}, u32[]{:S(2)}, u32[]{:S(2)}) %all-to-all-start) | async-done | bytes 262176 | tf_op jit(solution)/shard_map/all_to_all | solution.py:47
  27.9 2.2 %gather_fusion.1 = bf16[256,32,128]{2,1,0:T(8,128)(2,1)} fusion(bf16[32,32,128]{2,1,0:T(8,128)(2,1)S(1)} %bitcast.83, s32[1024]{0:T(1024)S(1)} %pad_clamp_fusion.1), kind=kCustom, calls=%fused_computation.1 | custom fusion | bytes 4195328 | tf_op jit(solution)/shard_map/gather | solution.py:48
  30.1 6.9 %fusion.16 = bf16[16,4,8,128]{3,2,1,0:T(8,128)(2,1)S(1)} fusion(bf16[16,16,128,128]{3,2,1,0:T(8,128)(2,1)} %param.7, bf16[16,16,32,128]{3,2,1,0:T(8,128)(2,1)} %bitcast.85, bf16[16,16,32,128]{3,2,1,0:T(8,128)(2,1)S(1)} %bitcast.84, pred[16,16]{1,0:T(8,128)(4,1)S(1)} %copy.40), kind=kOutput, calls=%fused_computation.20 | convolution fusion | flops 269549568 | bytes 12714240 | tf_op jit(solution)/shard_map/bkfj,bkij->fbi/dot_general | solution.py:53
  37.1 7.3 %all_gather.6 = bf16[128,2048]{1,0:T(8,128)(2,1)S(1)} all-gather(bf16[32,2048]{1,0:T(8,128)(2,1)S(1)} %bitcast.90), channel_id=1, replica_groups=mesh['rows'=8,'cols'=4] {'cols'}, dimensions={0}, use_global_device_ids=true | all-gather | bytes 655360 | tf_op jit(solution)/shard_map/all_gather | solution.py:58
  44.4 1.3 multiply_convert_fusion
  45.8 0.1 fusion.35
  45.9 0.2 select_reduce_fusion
  46.2 14.7 %all-gather.2.cloned.1.call-done = bf16[256,2048]{1,0:T(8,128)(2,1)} async-done(((bf16[64,2048]{1,0:T(8,128)(2,1)}), bf16[256,2048]{1,0:T(8,128)(2,1)}) %all-gather.2.cloned.1.call-update) | async-done | bytes 1048592 | tf_op jit(solution)/shard_map/all_gather | solution.py:68
  60.9 1.5 %fusion.15 = bf16[4,8,16,128]{3,1,2,0:T(8,128)(2,1)S(1)} fusion(bf16[256,2048]{1,0:T(8,128)(2,1)} %all-gather.2.cloned.1.call-done, bf16[128,256]{1,0:T(8,128)(2,1)S(1)} %copy-done, s32[]{:T(128)S(6)} %select_n.136), kind=kOutput, calls=%fused_computation.19 | convolution fusion | flops 33619968 | bytes 1196036 | tf_op jit(solution)/shard_map/dot_general | solution.py:69
  62.5 6.5 %fusion.28 = f32[16,32,16,128]{3,1,2,0:T(8,128)} fusion(bf16[16,16,128,128]{3,2,1,0:T(8,128)(2,1)} %param.7, bf16[32,16,128,1]{2,1,0,3:T(8,128)(2,1)S(1)} %bitcast.88), kind=kOutput, calls=%fused_computation.38 | convolution fusion | flops 268435456 | bytes 12713984 | tf_op jit(solution)/shard_map/fbi,bkij->bkfj/dot_general | solution.py:76
  69.0 10.2 %scatter_custom_fusion.2 = f32[17,4096]{1,0:T(8,128)S(1)} fusion(s32[256]{0:T(256)S(1)} %bitcast.99, f32[32,8,32,128]{3,2,1,0:T(8,128)} %bitcast.81, f32[]{:T(128)} %constant.69.clone.1), kind=kCustom, calls=%fused_computation.6 | custom fusion | flops 1048576 | bytes 4472836 | tf_op jit(solution)/shard_map/scatter-add | solution.py:101
  79.3 10.2 %scatter_custom_fusion = f32[33,4096]{1,0:T(8,128)S(1)} fusion(s32[256]{0:T(256)S(1)} %bitcast.98, f32[32,8,32,128]{3,2,1,0:T(8,128)} %bitcast.82, f32[]{:T(128)} %constant.69.clone.1), kind=kCustom, calls=%fused_computation.8 | custom fusion | flops 1048576 | bytes 4734980 | tf_op jit(solution)/shard_map/scatter-add | solution.py:85
  89.5 0.7 copy.63
  90.3 5.5 %all-to-all-start.1 = ((bf16[8,4,32,128]{3,2,1,0:T(8,128)(2,1)}), bf16[8,4,32,128]{3,2,1,0:T(8,128)(2,1)S(1)}, u32[]{:S(2)}, u32[]{:S(2)}) async-start(bf16[8,4,32,128]{3,2,1,0:T(8,128)(2,1)} %bitcast.37), calls=%async_computation.1 | async-start | bytes 524288 | tf_op jit(solution)/shard_map/all_to_all | solution.py:89
  95.8 0.4 fusion.45
  96.2 37.6 %psum.7 = f32[32,256]{1,0:T(8,128)S(1)} all-reduce(f32[32,256]{1,0:T(8,128)S(1)} %fusion.45), channel_id=1, replica_groups=mesh['rows'=8,'cols'=4] {'rows'}, use_global_device_ids=true, to_apply=%region_4.5 | all-reduce | flops 8192 | bytes 65536 | tf_op jit(solution)/shard_map/psum | solution.py:74
  133.8 0.6 broadcast_multiply_fusion
  134.4 1.7 %scatter_custom_fusion.1 = f32[17,4096]{1,0:T(8,128)S(1)} fusion(s32[32]{0:T(128)S(1)} %reshape.376, f32[4,8,32,128]{3,2,1,0:T(8,128)S(1)} %bitcast_convert_fusion, f32[]{:T(128)} %constant.69.clone.1), kind=kCustom, calls=%fused_computation.21 | custom fusion | flops 131072 | bytes 802820 | tf_op jit(solution)/shard_map/scatter-add | solution.py:97
  136.2 0.7 copy.84
  (36 shorter events, 1.2 us)
Async XLA Ops:
  7.2 37.3 %copy-start = (bf16[128,256]{1,0:T(8,128)(2,1)S(1)}, bf16[128,256]{1,0:T(8,128)(2,1)}, u32[]{:S(2)}) copy-start(bf16[128,256]{1,0:T(8,128)(2,1)} %param.8) | copy-start | bytes 196612
  11.7 16.2 %all-to-all-start = ((bf16[8,4,32,128]{3,2,1,0:T(8,128)(2,1)}), bf16[8,4,32,128]{3,2,1,0:T(8,128)(2,1)S(1)}, u32[]{:S(2)}, u32[]{:S(2)}) async-start(bf16[8,4,32,128]{3,2,1,0:T(8,128)(2,1)} %copy.44), calls=%async_computation | async-start | bytes 524288 | tf_op jit(solution)/shard_map/all_to_all | solution.py:47
  19.0 41.9 %all-gather.2.cloned.1.call-start = ((), (), s32[]{:S(2)}) async-start(), calls=%async_computation.2 | async-start | bytes 1310720 | tf_op jit(solution)/shard_map/all_gather | solution.py:68
  30.1 14.3 %copy-start.2 = (bf16[64,2048]{1,0:T(8,128)(2,1)S(1)}, bf16[64,2048]{1,0:T(8,128)(2,1)}, u32[]{:S(2)}) copy-start(bf16[64,2048]{1,0:T(8,128)(2,1)} %param.9) | copy-start | bytes 786436
  79.3 16.5 %copy-start.1 = (bf16[256,2048]{1,0:T(8,128)(2,1)S(1)}, bf16[256,2048]{1,0:T(8,128)(2,1)}, u32[]{:S(2)}) copy-start(bf16[256,2048]{1,0:T(8,128)(2,1)} %all-gather.2.cloned.1.call-done) | copy-start | bytes 3145732
  90.3 44.1 %all-to-all-start.1 = ((bf16[8,4,32,128]{3,2,1,0:T(8,128)(2,1)}), bf16[8,4,32,128]{3,2,1,0:T(8,128)(2,1)S(1)}, u32[]{:S(2)}, u32[]{:S(2)}) async-start(bf16[8,4,32,128]{3,2,1,0:T(8,128)(2,1)} %bitcast.37), calls=%async_computation.1 | async-start | bytes 524288 | tf_op jit(solution)/shard_map/all_to_all | solution.py:89
Sparse Core Ops, SparseCore 0:
  45.9 15.0 all-gather.1
where the time goes:
time: 144 us
  blocking collectives  44.9 us (31%)
  other arithmetic  24.7 us (17%)
  waiting for transfers between devices  19.3 us (13%)
  matrix products  16.9 us (12%)
  between operations  14.2 us (10%)
  starting transfers between devices  12.9 us (9%)
  local copies, waits for them, and re-layouts  10.8 us (8%)
    psum x1, blocking collectives, body(): weight_grad = lax.psum(block_grad, 'rows') * grad_scale  37.6 us
    all_gather x1, waiting for transfers between devices, body(): portion = lax.all_gather(pre_grad, 'cols', axis=0, tiled=True)  14.7 us
    scatter-add x1, other arithmetic, body(): jax.ops.segment_sum(contrib_flat, self_target, num_segments=blocks_n + 1)  10.2 us
    scatter-add x1, other arithmetic, body(): jax.ops.segment_sum(contrib_flat, send_target, num_segments=slot_total + 1)  10.2 us
    all_gather x1, blocking collectives, body(): lax.all_gather(aggregated, 'cols', axis=0, tiled=True)  7.35 us
    all_to_all x1, starting transfers between devices, body(): lax.all_to_all(outgoing, 'rows', split_axis=0, concat_axis=0, tiled=True)  7.31 us
    dot_general x1, matrix products, body(): jnp.einsum('bkfj,bkij->fbi', picked, adj_weight, preferred_element_type=j...  6.91 us
    dot_general x1, matrix products, body(): jnp.einsum('fbi,bkij->bkfj', agg_grad.reshape(feat_rows, blocks_n, tile_n...  6.54 us
  transfers between devices with their start and end apart: 3, of which 2 were waited for; matrix products, arithmetic and copies ran while one was open for 4% of the time, Pallas kernels for 0%

commit v1 on v0

--- a/solution.py
+++ b/solution.py
@@ -5,6 +5,17 @@
 from jax.sharding import PartitionSpec as P
 
 CAP = 4
+
+
+def gather_by_hops(shard, axis, along):
+    size = lax.axis_size(axis)
+    route = [(i, (i + 1) % size) for i in range(size)]
+    terms = [shard]
+    for far in range(1, size):
+        terms = [lax.ppermute(terms[0], axis, route), *terms]
+    result = jnp.concatenate(terms, axis=along)
+    shift = (lax.axis_index(axis) + 1) * terms[-1].shape[along]
+    return jnp.roll(result, shift, axis=along)
 
 
 def body(feats_t, adj_index, adj_weight, weight, cotangent_t):
@@ -65,7 +76,7 @@
         jnp.bfloat16
     )
     w_mine = lax.dynamic_slice_in_dim(weight, col_pos * feat_rows, feat_rows, 0)
-    portion = lax.all_gather(pre_grad, "cols", axis=0, tiled=True)
+    portion = gather_by_hops(pre_grad, "cols", 0)
     grad_acc = jnp.dot(w_mine, portion, preferred_element_type=jnp.float32)
     block_grad = lax.dot_general(
         aggregated, portion, (((1,), (1,)), ((), ())), preferred_element_type=jnp.float32

time: 144 us -> 130 us (0.903)
  between operations: 14.2 us -> 0.93 us
  waiting for transfers between devices: 19.3 us -> 22.1 us
  starting transfers between devices: 12.9 us -> 11.3 us
    ppermute x0 -> x3, waiting for transfers between devices: none -> 16.6 us  [gather_by_hops(): terms = [lax.ppermute(terms[0], axis, route), *terms]]
    all_gather x1 -> x0, waiting for transfers between devices: 14.7 us -> none  [body(): portion = lax.all_gather(pre_grad, 'cols', axis=0, tiled=True)]
    all_to_all x1, starting transfers between devices: 5.52 us -> 3.59 us  [body(): lax.all_to_all(sending.astype(jnp.bfloat16), 'rows', split_axis=0, concat...]
  transfers between devices with their start and end apart: 3 -> 5, of which waited for: 2 -> 4; matrix products, arithmetic and copies ran while one was open for 4% -> 4% of each run, Pallas kernels for 0% -> 0%
where the time goes in v1:
time: 130 us; the launch traced here: 129 us
  blocking collectives  44.7 us (34%)
  other arithmetic  24.7 us (19%)
  waiting for transfers between devices  22.1 us (17%)
  matrix products  15.6 us (12%)
  starting transfers between devices  11.3 us (9%)
  local copies, waits for them, and re-layouts  10.1 us (8%)
    psum x1, blocking collectives, body(): weight_grad = lax.psum(block_grad, 'rows') * grad_scale  37.6 us
    ppermute x3, waiting for transfers between devices, gather_by_hops(): terms = [lax.ppermute(terms[0], axis, route), *terms]  16.6 us
    scatter-add x1, other arithmetic, body(): jax.ops.segment_sum(contrib_flat, self_target, num_segments=blocks_n + 1)  10.2 us
    scatter-add x1, other arithmetic, body(): jax.ops.segment_sum(contrib_flat, send_target, num_segments=slot_total + 1)  10.1 us
    all_to_all x1, starting transfers between devices, body(): lax.all_to_all(outgoing, 'rows', split_axis=0, concat_axis=0, tiled=True)  7.31 us
    all_gather x1, blocking collectives, body(): lax.all_gather(aggregated, 'cols', axis=0, tiled=True)  7.17 us
    dot_general x1, matrix products, body(): jnp.einsum('bkfj,bkij->fbi', picked, adj_weight, preferred_element_type=j...  6.91 us
    dot_general x1, matrix products, body(): jnp.einsum('fbi,bkij->bkfj', agg_grad.reshape(feat_rows, blocks_n, tile_n...  6.54 us
  transfers between devices with their start and end apart: 5, of which 4 were waited for; matrix products, arithmetic and copies ran while one was open for 4% of the time, Pallas kernels for 0%

profile of v1, /device:TPU:0, one launch (start us, length us, event | category | flops | bytes accessed | tf_op | source)
XLA Modules:
  0.0 129.3 jit_solution(928511400323275207)
XLA Ops:
  0.7 0.8 copy.41
  1.5 0.8 fusion.42
  2.8 0.3 compare_reduce_fusion
  3.2 0.2 reduce_window_sum.17
  3.3 0.9 copy.60
  4.3 0.2 convolution_convert_fusion.1
  4.5 0.7 copy.44
  5.2 7.3 %all-to-all-start = ((bf16[8,4,32,128]{3,2,1,0:T(8,128)(2,1)}), bf16[8,4,32,128]{3,2,1,0:T(8,128)(2,1)S(1)}, u32[]{:S(2)}, u32[]{:S(2)}) async-start(bf16[8,4,32,128]{3,2,1,0:T(8,128)(2,1)} %copy.44), calls=%async_computation | async-start | bytes 524288 | tf_op jit(solution)/shard_map/all_to_all | solution.py:58
  12.6 0.2 reduce_window_sum.18
  12.9 1.9 %gather_fusion = s32[256]{0:T(256)S(1)} fusion(s32[128]{0:T(128)S(1)} %sub.27, s32[1024]{0:T(1024)S(1)} %pad_clamp_fusion.2), kind=kCustom, calls=%fused_computation | custom fusion | bytes 3072 | tf_op jit(solution)/shard_map/gather | solution.py:50
  14.9 1.0 gather_fusion.2
  15.9 5.5 %all-to-all-done = bf16[8,4,32,128]{3,2,1,0:T(8,128)(2,1)S(1)} async-done(((bf16[8,4,32,128]{3,2,1,0:T(8,128)(2,1)}), bf16[8,4,32,128]{3,2,1,0:T(8,128)(2,1)S(1)}, u32[]{:S(2)}, u32[]{:S(2)}) %all-to-all-start) | async-done | bytes 262176 | tf_op jit(solution)/shard_map/all_to_all | solution.py:58
  21.4 2.2 %gather_fusion.1 = bf16[256,32,128]{2,1,0:T(8,128)(2,1)} fusion(bf16[32,32,128]{2,1,0:T(8,128)(2,1)S(1)} %bitcast.81, s32[1024]{0:T(1024)S(1)} %pad_clamp_fusion.1), kind=kCustom, calls=%fused_computation.1 | custom fusion | bytes 4195328 | tf_op jit(solution)/shard_map/gather | solution.py:59
  23.7 6.9 %fusion.16 = bf16[16,4,8,128]{3,2,1,0:T(8,128)(2,1)S(1)} fusion(bf16[16,16,128,128]{3,2,1,0:T(8,128)(2,1)} %param.7, bf16[16,16,32,128]{3,2,1,0:T(8,128)(2,1)} %bitcast.83, bf16[16,16,32,128]{3,2,1,0:T(8,128)(2,1)S(1)} %bitcast.82, pred[16,16]{1,0:T(8,128)(4,1)S(1)} %copy.40), kind=kOutput, calls=%fused_computation.20 | convolution fusion | flops 269549568 | bytes 12714240 | tf_op jit(solution)/shard_map/bkfj,bkij->fbi/dot_general | solution.py:64
  30.6 7.2 %all_gather.3 = bf16[128,2048]{1,0:T(8,128)(2,1)S(1)} all-gather(bf16[32,2048]{1,0:T(8,128)(2,1)S(1)} %bitcast.88), channel_id=1, replica_groups=mesh['rows'=8,'cols'=4] {'cols'}, dimensions={0}, use_global_device_ids=true | all-gather | bytes 655360 | tf_op jit(solution)/shard_map/all_gather | solution.py:69
  37.8 1.2 multiply_convert_fusion
  39.0 0.3 collective-permute-start
  39.3 5.4 %collective-permute-done = bf16[64,2048]{1,0:T(8,128)(2,1)S(1)} collective-permute-done((bf16[64,2048]{1,0:T(8,128)(2,1)S(1)}, bf16[64,2048]{1,0:T(8,128)(2,1)S(1)}, u32[]{:S(2)}, u32[]{:S(2)}) %collective-permute-start) | collective-permute-done | bytes 262176 | tf_op jit(solution)/shard_map/ppermute | solution.py:15
  44.9 5.7 %collective-permute-done.1 = bf16[64,2048]{1,0:T(8,128)(2,1)S(1)} collective-permute-done((bf16[64,2048]{1,0:T(8,128)(2,1)S(1)}, bf16[64,2048]{1,0:T(8,128)(2,1)S(1)}, u32[]{:S(2)}, u32[]{:S(2)}) %collective-permute-start.1) | collective-permute-done | bytes 262176 | tf_op jit(solution)/shard_map/ppermute | solution.py:15
  50.6 0.1 fusion.38
  50.9 5.5 %collective-permute-done.2 = bf16[64,2048]{1,0:T(8,128)(2,1)S(1)} collective-permute-done((bf16[64,2048]{1,0:T(8,128)(2,1)S(1)}, bf16[64,2048]{1,0:T(8,128)(2,1)S(1)}, u32[]{:S(2)}, u32[]{:S(2)}) %collective-permute-start.2) | collective-permute-done | bytes 262176 | tf_op jit(solution)/shard_map/ppermute | solution.py:15
  56.6 0.3 fusion.15
  56.9 6.5 %fusion.31 = f32[16,32,16,128]{3,1,2,0:T(8,128)} fusion(bf16[16,16,128,128]{3,2,1,0:T(8,128)(2,1)} %param.7, bf16[32,16,128,1]{2,1,0,3:T(8,128)(2,1)S(1)} %bitcast.86), kind=kOutput, calls=%fused_computation.41 | convolution fusion | flops 268435456 | bytes 12713984 | tf_op jit(solution)/shard_map/fbi,bkij->bkfj/dot_general | solution.py:87
  63.5 10.2 %scatter_custom_fusion.2 = f32[17,4096]{1,0:T(8,128)S(1)} fusion(s32[256]{0:T(256)S(1)} %bitcast.97, f32[32,8,32,128]{3,2,1,0:T(8,128)} %bitcast.79, f32[]{:T(128)} %constant.90.clone.1), kind=kCustom, calls=%fused_computation.6 | custom fusion | flops 1048576 | bytes 4472836 | tf_op jit(solution)/shard_map/scatter-add | solution.py:112
  73.7 10.1 %scatter_custom_fusion = f32[33,4096]{1,0:T(8,128)S(1)} fusion(s32[256]{0:T(256)S(1)} %bitcast.96, f32[32,8,32,128]{3,2,1,0:T(8,128)} %bitcast.80, f32[]{:T(128)} %constant.90.clone.1), kind=kCustom, calls=%fused_computation.8 | custom fusion | flops 1048576 | bytes 4734980 | tf_op jit(solution)/shard_map/scatter-add | solution.py:96
  83.9 0.7 copy.63
  84.6 3.6 %all-to-all-start.1 = ((bf16[8,4,32,128]{3,2,1,0:T(8,128)(2,1)}), bf16[8,4,32,128]{3,2,1,0:T(8,128)(2,1)S(1)}, u32[]{:S(2)}, u32[]{:S(2)}) async-start(bf16[8,4,32,128]{3,2,1,0:T(8,128)(2,1)} %bitcast.37), calls=%async_computation.1 | async-start | bytes 524288 | tf_op jit(solution)/shard_map/all_to_all | solution.py:100
  88.2 0.4 fusion.20
  88.6 37.6 %psum.7 = f32[32,256]{1,0:T(8,128)S(1)} all-reduce(f32[32,256]{1,0:T(8,128)S(1)} %fusion.20), channel_id=1, replica_groups=mesh['rows'=8,'cols'=4] {'rows'}, use_global_device_ids=true, to_apply=%region_4.5 | all-reduce | flops 8192 | bytes 65536 | tf_op jit(solution)/shard_map/psum | solution.py:85
  126.2 0.6 broadcast_multiply_fusion
  126.9 1.7 %scatter_custom_fusion.1 = f32[17,4096]{1,0:T(8,128)S(1)} fusion(s32[32]{0:T(128)S(1)} %reshape.376, f32[4,8,32,128]{3,2,1,0:T(8,128)S(1)} %bitcast_convert_fusion, f32[]{:T(128)} %constant.90.clone.1), kind=kCustom, calls=%fused_computation.24 | custom fusion | flops 131072 | bytes 802820 | tf_op jit(solution)/shard_map/scatter-add | solution.py:108
  128.6 0.7 copy.84
  (47 shorter events, 1.6 us)
Async XLA Ops:
  0.6 37.1 %copy-start = (bf16[128,256]{1,0:T(8,128)(2,1)S(1)}, bf16[128,256]{1,0:T(8,128)(2,1)}, u32[]{:S(2)}) copy-start(bf16[128,256]{1,0:T(8,128)(2,1)} %param.8) | copy-start | bytes 196612
  0.6 14.2 %copy-start.1 = (bf16[32,2048]{1,0:T(8,128)(2,1)S(1)}, bf16[32,2048]{1,0:T(8,128)(2,1)}, u32[]{:S(2)}) copy-start(bf16[32,2048]{1,0:T(8,128)(2,1)} %param.5) | copy-start | bytes 393220
  5.2 16.2 %all-to-all-start = ((bf16[8,4,32,128]{3,2,1,0:T(8,128)(2,1)}), bf16[8,4,32,128]{3,2,1,0:T(8,128)(2,1)S(1)}, u32[]{:S(2)}, u32[]{:S(2)}) async-start(bf16[8,4,32,128]{3,2,1,0:T(8,128)(2,1)} %copy.44), calls=%async_computation | async-start | bytes 524288 | tf_op jit(solution)/shard_map/all_to_all | solution.py:58
  23.7 14.1 %copy-start.2 = (bf16[64,2048]{1,0:T(8,128)(2,1)S(1)}, bf16[64,2048]{1,0:T(8,128)(2,1)}, u32[]{:S(2)}) copy-start(bf16[64,2048]{1,0:T(8,128)(2,1)} %param.9) | copy-start | bytes 786436
  39.0 5.8 %collective-permute-start = (bf16[64,2048]{1,0:T(8,128)(2,1)S(1)}, bf16[64,2048]{1,0:T(8,128)(2,1)S(1)}, u32[]{:S(2)}, u32[]{:S(2)}) collective-permute-start(bf16[64,2048]{1,0:T(8,128)(2,1)S(1)} %get-tuple-element.10), channel_id=1, source_target_pairs={{0,1},{1,2},{2,3},{3,0},{4,5},{5,6},{6,7},{7,4},{8,9},{9,10},{10,1... | collective-permute-start | bytes 786440 | tf_op jit(solution)/shard_map/ppermute | solution.py:15
  44.8 5.8 %collective-permute-start.1 = (bf16[64,2048]{1,0:T(8,128)(2,1)S(1)}, bf16[64,2048]{1,0:T(8,128)(2,1)S(1)}, u32[]{:S(2)}, u32[]{:S(2)}) collective-permute-start(bf16[64,2048]{1,0:T(8,128)(2,1)S(1)} %collective-permute-done), channel_id=1, source_target_pairs={{0,1},{1,2},{2,3},{3,0},{4,5},{5,6},{6,7},{7,4},{8,9},{9,10},{10,1... | collective-permute-start | bytes 786440 | tf_op jit(solution)/shard_map/ppermute | solution.py:15
  50.6 5.8 %collective-permute-start.2 = (bf16[64,2048]{1,0:T(8,128)(2,1)S(1)}, bf16[64,2048]{1,0:T(8,128)(2,1)S(1)}, u32[]{:S(2)}, u32[]{:S(2)}) collective-permute-start(bf16[64,2048]{1,0:T(8,128)(2,1)S(1)} %collective-permute-done.1), channel_id=1, source_target_pairs={{0,1},{1,2},{2,3},{3,0},{4,5},{5,6},{6,7},{7,4},{8,9},{9,10},{10,1... | collective-permute-start | bytes 786440 | tf_op jit(solution)/shard_map/ppermute | solution.py:15
  84.6 42.2 %all-to-all-start.1 = ((bf16[8,4,32,128]{3,2,1,0:T(8,128)(2,1)}), bf16[8,4,32,128]{3,2,1,0:T(8,128)(2,1)S(1)}, u32[]{:S(2)}, u32[]{:S(2)}) async-start(bf16[8,4,32,128]{3,2,1,0:T(8,128)(2,1)} %bitcast.37), calls=%async_computation.1 | async-start | bytes 524288 | tf_op jit(solution)/shard_map/all_to_all | solution.py:100
